TPU v7x, 256 devices: a whole 4x4x8 slice. The times are simulated.
256 devices in a mesh: dp: 8 (over x, core), tm: 32 (over z, y).
Axes of the slice: x: 4, y: 4, z: 8, core: 2. Of those that a mesh axis runs over, the one named last changes fastest.
Arguments:
- latents: bfloat16 [8, 17, 64, 64, 256], P('dp', None, 'tm'), may hold values from -6 to 6
- cotangent: bfloat16 [8, 17, 64, 64, 256], P('dp', None, 'tm'), may hold values from -6 to 6
- spatial_weight: bfloat16 [3, 3, 256, 256], replicated, may hold values from -0.125 to 0.125
- temporal_weight: bfloat16 [3, 256, 256], replicated, may hold values from -0.21875 to 0.21875
Outputs:
- block_out: bfloat16 [8, 17, 64, 64, 256], P('dp', None, 'tm')
- latents_grad: bfloat16 [8, 17, 64, 64, 256], P('dp', None, 'tm')
- spatial_grad: float32 [3, 3, 256, 256], replicated
- temporal_grad: float32 [3, 256, 256], replicated
All inputs are finite; a program needn't handle non-finite values.
Results may differ from a plain program's by a relative error of at most 0.0085.
Values may be sent and summed in bfloat16 or wider, within the bound.
A program may use at most 64 MiB of HBM per device.

v0:
```python
import jax
import jax.numpy as jnp
from jax import lax
from jax.sharding import PartitionSpec as P


def with_halo(cells, sides, width):
    for axis, dim in sides:
        count = lax.axis_size(axis)
        ends = count - 1
        head = lax.slice_in_dim(cells, 0, width, axis=dim)
        tail = lax.slice_in_dim(cells, cells.shape[dim] - width, cells.shape[dim], axis=dim)
        cells = jnp.concatenate(
            [
                lax.ppermute(tail, axis, [(i, (i + 1) % count) for i in range(ends)]),
                cells,
                lax.ppermute(head, axis, [((i + 1) % count, i) for i in range(ends)]),
            ],
            axis=dim,
        )
    return cells


def band_patches(extended, rows_out, flipped):
    padded = jnp.pad(extended, ((0, 0), (0, 0), (1, 1), (0, 0)))
    cols = extended.shape[2]
    pieces = []
    for first in range(3):
        for second in range(3):
            top = 2 - first if flipped else first
            left = 2 - second if flipped else second
            pieces.append(padded[:, top : top + rows_out, left : left + cols, :])
    return jnp.concatenate(pieces, axis=3).reshape(-1, 9 * extended.shape[3])


def causal_mix(act, weight):
    clips, frames, cells, chans = act.shape
    padded = jnp.pad(act, ((0, 0), (2, 0), (0, 0), (0, 0)))
    total = jnp.zeros((clips * frames * cells, chans), jnp.float32)
    for tap in range(3):
        earlier = padded[:, 2 - tap : 2 - tap + frames].reshape(-1, chans)
        total = total + jnp.dot(earlier, weight[tap], preferred_element_type=jnp.float32)
    return total.astype(jnp.bfloat16)


def anti_mix(cot, weight):
    clips, frames, cells, chans = cot.shape
    padded = jnp.pad(cot, ((0, 0), (0, 2), (0, 0), (0, 0)))
    total = jnp.zeros((clips * frames * cells, chans), jnp.float32)
    for tap in range(3):
        later = padded[:, tap : tap + frames].reshape(-1, chans)
        total = total + lax.dot_general(
            later, weight[tap], (((1,), (1,)), ((), ())), preferred_element_type=jnp.float32
        )
    return total.astype(jnp.bfloat16)


def tap_grads(act, cot):
    clips, frames, cells, chans = act.shape
    padded = jnp.pad(act, ((0, 0), (2, 0), (0, 0), (0, 0)))
    cot_flat = cot.reshape(-1, chans)
    parts = []
    for tap in range(3):
        earlier = padded[:, 2 - tap : 2 - tap + frames].reshape(-1, chans)
        parts.append(
            lax.dot_general(
                earlier, cot_flat, (((0,), (0,)), ((), ())), preferred_element_type=jnp.float32
            )
        )
    return jnp.stack(parts)


def silu_grad(act_grad, pre):
    sig = jax.nn.sigmoid(pre)
    return (act_grad.astype(jnp.float32) * sig * (1.0 + pre * (1.0 - sig))).astype(jnp.bfloat16)


def body(latents, cotangent, spatial_weight, temporal_weight):
    clips, frames, rows, cols, chans = latents.shape
    flat_w = spatial_weight.reshape(9 * chans, chans)
    flip_w = jnp.transpose(spatial_weight, (0, 1, 3, 2)).reshape(9 * chans, chans)
    cot_band = cotangent.reshape(clips, frames, rows * cols, chans)
    extended = with_halo(latents, (("tm", 2),), 1)
    patches = band_patches(extended.reshape(clips * frames, rows + 2, cols, chans), rows, False)
    pre = jnp.dot(patches, flat_w, preferred_element_type=jnp.float32)
    act = jax.nn.silu(pre).astype(jnp.bfloat16).reshape(clips, frames, rows * cols, chans)
    mixed = causal_mix(act, temporal_weight)
    act_grad = anti_mix(cot_band, temporal_weight)
    pre_grad = silu_grad(act_grad, pre)
    grad_ext = with_halo(pre_grad.reshape(clips, frames, rows, cols, chans), (("tm", 2),), 1)
    back = jnp.dot(
        band_patches(grad_ext.reshape(clips * frames, rows + 2, cols, chans), rows, True),
        flip_w,
        preferred_element_type=jnp.float32,
    )
    temporal_local = tap_grads(act, cot_band)
    block_out = (latents.reshape(-1, chans).astype(jnp.float32) + mixed.astype(jnp.float32)).astype(
        jnp.bfloat16
    )
    latents_grad = (cotangent.reshape(-1, chans).astype(jnp.float32) + back).astype(jnp.bfloat16)
    spatial_local = lax.dot_general(
        patches, pre_grad, (((0,), (0,)), ((), ())), preferred_element_type=jnp.float32
    )
    spatial_sum, temporal_sum = lax.psum((spatial_local, temporal_local), ("dp", "tm"))
    scale = (clips * lax.axis_size("dp") * frames * rows * lax.axis_size("tm") * cols) ** (-0.5)
    return (
        block_out.reshape(latents.shape),
        latents_grad.reshape(latents.shape),
        (spatial_sum * scale).reshape(3, 3, chans, chans),
        temporal_sum * scale,
    )


def solution(mesh):
    in_specs = (P("dp", None, "tm", None, None), P("dp", None, "tm", None, None), P(), P())
    out_specs = (P("dp", None, "tm", None, None), P("dp", None, "tm", None, None), P(), P())
    return jax.shard_map(body, mesh=mesh, in_specs=in_specs, out_specs=out_specs, check_vma=False)
```

profile of v0, /device:TPU:2, one launch (start us, length us, event | category | flops | bytes accessed | tf_op | source)
XLA Modules:
  0.0 338.0 jit_solution(11071545228273672446)
XLA Ops:
  7.2 0.0 copy-start
  7.2 0.0 all-reduce.7.cloned.1.call-start
  7.2 2.4 fusion.37
  9.6 4.4 %collective-permute-start = (bf16[1,17,1,64,256]{4,3,2,1,0:T(8,128)(2,1)}, bf16[1,17,1,64,256]{4,3,2,1,0:T(8,128)(2,1)}, u32[]{:S(2)}, u32[]{:S(2)}) collective-permute-start(bf16[1,17,1,64,256]{4,3,2,1,0:T(8,128)(2,1)} %get-tuple-element.12), channel_id=1, source_target_pairs={{0,1},{1,2},{2,3},{3,4},{4,5},{5,6},{6,7},{7,8},{8,9},{9,10},{10,1... | collective-permute-start | bytes 1671176 | tf_op jit(solution)/shard_map/ppermute | solution.py:15
  14.1 1.3 collective-permute-start.1
  15.4 0.0 copy-done
  15.4 2.8 fusion.26
  18.1 0.0 copy-done.6
  18.1 1.5 copy.8
  19.7 0.2 pad_slice_fusion.12
  19.9 1.4 copy-done.3
  21.3 0.0 copy-done.8
  21.3 0.5 convolution_add_fusion.1
  21.8 3.6 %collective-permute-done = bf16[1,17,1,64,256]{4,3,2,1,0:T(8,128)(2,1)} collective-permute-done((bf16[1,17,1,64,256]{4,3,2,1,0:T(8,128)(2,1)}, bf16[1,17,1,64,256]{4,3,2,1,0:T(8,128)(2,1)}, u32[]{:S(2)}, u32[]{:S(2)}) %collective-permute-start) | collective-permute-done | bytes 557088 | tf_op jit(solution)/shard_map/ppermute | solution.py:15
  25.4 4.9 %collective-permute-done.1 = bf16[1,17,1,64,256]{4,3,2,1,0:T(8,128)(2,1)} collective-permute-done((bf16[1,17,1,64,256]{4,3,2,1,0:T(8,128)(2,1)}, bf16[1,17,1,64,256]{4,3,2,1,0:T(8,128)(2,1)}, u32[]{:S(2)}, u32[]{:S(2)}) %collective-permute-start.1) | collective-permute-done | bytes 557088 | tf_op jit(solution)/shard_map/ppermute | solution.py:17
  30.4 0.0 copy-done.1
  30.4 1.5 maximum_bitcast_fusion
  31.8 0.4 fusion.10
  32.2 0.1 slice_dynamic-update-slice_fusion.5
  32.3 0.6 fusion.11
  32.9 0.7 fusion.12
  33.6 0.1 slice_dynamic-update-slice_fusion.4
  33.7 0.6 fusion.13
  34.3 0.7 fusion.14
  35.0 0.1 slice_dynamic-update-slice_fusion.3
  35.1 0.6 fusion.15
  35.7 2.9 multiply_convert_fusion
  38.6 0.5 convolution_bitcast_fusion.2
  39.1 1.8 fusion.28
  41.0 1.0 fusion.9
  42.0 0.0 copy-start.4
  42.0 4.4 %fusion.38 = f32[2304,256]{1,0:T(8,128)} fusion(bf16[2176,2304]{1,0:T(8,128)(2,1)S(1)} %bitcast.83, bf16[2176,256]{1,0:T(8,128)(2,1)S(1)} %fusion.9), kind=kOutput, calls=%fused_computation.75 | convolution fusion | flops 2566914048 | bytes 13500416 | tf_op jit(solution)/shard_map/dot_general | solution.py:101
  46.4 0.0 copy-done.4
  46.4 1.2 fusion.36
  47.6 3.5 %collective-permute-start.2 = (bf16[1,17,1,64,256]{4,3,2,1,0:T(8,128)(2,1)}, bf16[1,17,1,64,256]{4,3,2,1,0:T(8,128)(2,1)}, u32[]{:S(2)}, u32[]{:S(2)}) collective-permute-start(bf16[1,17,1,64,256]{4,3,2,1,0:T(8,128)(2,1)} %get-tuple-element.6), channel_id=1, source_target_pairs={{0,1},{1,2},{2,3},{3,4},{4,5},{5,6},{6,7},{7,8},{8,9},{9,10},{10,1... | collective-permute-start | bytes 1671176 | tf_op jit(solution)/shard_map/ppermute | solution.py:15
  51.2 1.3 collective-permute-start.3
  52.4 0.1 pad_slice_fusion.14
  52.6 0.0 copy-start.2
  52.6 0.5 convolution_bitcast_fusion
  53.1 0.5 convolution_bitcast_fusion.1
  53.6 0.0 copy-done.2
  53.6 0.9 pad_maximum_fusion
  54.6 0.0 all-reduce.7.cloned.1.call-update
  54.6 2.5 convolution_add_fusion.3
  57.1 0.0 copy-start.5
  57.1 2.5 fusion.4
  59.6 1.8 collective-permute-done.2
  61.4 4.9 %collective-permute-done.3 = bf16[1,17,1,64,256]{4,3,2,1,0:T(8,128)(2,1)} collective-permute-done((bf16[1,17,1,64,256]{4,3,2,1,0:T(8,128)(2,1)}, bf16[1,17,1,64,256]{4,3,2,1,0:T(8,128)(2,1)}, u32[]{:S(2)}, u32[]{:S(2)}) %collective-permute-start.3) | collective-permute-done | bytes 557088 | tf_op jit(solution)/shard_map/ppermute | solution.py:17
  66.3 0.0 copy-done.5
  66.3 1.5 maximum_bitcast_fusion.1
  67.8 0.3 fusion.16
  68.1 0.1 slice_dynamic-update-slice_fusion.2
  68.3 0.7 fusion.17
  69.0 0.6 fusion.18
  69.6 0.1 slice_dynamic-update-slice_fusion.1
  69.7 0.7 fusion.19
  70.4 0.6 fusion.20
  71.0 0.1 slice_dynamic-update-slice_fusion
  71.1 0.7 fusion.21
  71.8 0.6 copy-done.7
  72.3 3.8 %fusion = bf16[2176,256]{1,0:T(8,128)(2,1)} fusion(bf16[2176,2304]{1,0:T(8,128)(2,1)S(1)} %bitcast.84, bf16[2304,256]{1,0:T(8,128)(2,1)S(1)} %bitcast.79, bf16[2176,256]{1,0:T(8,128)(2,1)S(1)} %bitcast.67), kind=kOutput, calls=%fused_computation.5 | convolution fusion | flops 2568585216 | bytes 13434880 | tf_op jit(solution)/shard_map/dot_general | solution.py:91
  76.1 250.7 %all-reduce.7.cloned.1.call-done = (f32[2304,256]{1,0:T(8,128)}, f32[3,256,256]{2,1,0:T(8,128)}) async-done(((f32[2304,256]{1,0:T(8,128)}, f32[3,256,256]{2,1,0:T(8,128)}), (f32[2304,256]{1,0:T(8,128)}, f32[3,256,256]{2,1,0:T(8,128)})) %all-reduce.7.cloned.1.call-update) | async-done | bytes 3145744 | tf_op jit(solution)/shard_map/psum | solution.py:104
  326.8 3.3 broadcast_multiply_fusion
  330.2 0.9 broadcast_multiply_fusion.1
  (7 shorter events, 0.0 us)
Async XLA Ops:
  7.2 8.2 %copy-start = (bf16[1,17,2,64,256]{4,3,2,1,0:T(8,128)(2,1)S(1)}, bf16[1,17,2,64,256]{4,3,2,1,0:T(8,128)(2,1)}, u32[]{:S(2)}) copy-start(bf16[1,17,2,64,256]{4,3,2,1,0:T(8,128)(2,1)} %param.5) | copy-start | bytes 3342340
  7.2 319.6 %all-reduce.7.cloned.1.call-start = ((), (), s32[]{:S(2)}) async-start(), calls=%async_computation | async-start | bytes 6291456 | tf_op jit(solution)/shard_map/psum | solution.py:104
  9.6 8.5 %copy-start.6 = (bf16[3,3,256,256]{3,2,1,0:T(8,128)(2,1)S(1)}, bf16[3,3,256,256]{3,2,1,0:T(8,128)(2,1)}, u32[]{:S(2)}) copy-start(bf16[3,3,256,256]{3,2,1,0:T(8,128)(2,1)} %param.6) | copy-start | bytes 3538948
  9.6 15.8 %collective-permute-start = (bf16[1,17,1,64,256]{4,3,2,1,0:T(8,128)(2,1)}, bf16[1,17,1,64,256]{4,3,2,1,0:T(8,128)(2,1)}, u32[]{:S(2)}, u32[]{:S(2)}) collective-permute-start(bf16[1,17,1,64,256]{4,3,2,1,0:T(8,128)(2,1)} %get-tuple-element.12), channel_id=1, source_target_pairs={{0,1},{1,2},{2,3},{3,4},{4,5},{5,6},{6,7},{7,8},{8,9},{9,10},{10,1... | collective-permute-start | bytes 1671176 | tf_op jit(solution)/shard_map/ppermute | solution.py:15
  14.1 16.3 %collective-permute-start.1 = (bf16[1,17,1,64,256]{4,3,2,1,0:T(8,128)(2,1)}, bf16[1,17,1,64,256]{4,3,2,1,0:T(8,128)(2,1)}, u32[]{:S(2)}, u32[]{:S(2)}) collective-permute-start(bf16[1,17,1,64,256]{4,3,2,1,0:T(8,128)(2,1)} %get-tuple-element.13), channel_id=1, source_target_pairs={{1,0},{2,1},{3,2},{4,3},{5,4},{6,5},{7,6},{8,7},{9,8},{10,9},{11,1... | collective-permute-start | bytes 1671176 | tf_op jit(solution)/shard_map/ppermute | solution.py:17
  19.7 1.6 copy-start.3
  19.7 1.7 copy-start.8
  21.3 9.0 %copy-start.1 = (bf16[1,17,2,64,256]{4,3,2,1,0:T(8,128)(2,1)S(1)}, bf16[1,17,2,64,256]{4,3,2,1,0:T(8,128)(2,1)}, u32[]{:S(2)}) copy-start(bf16[1,17,2,64,256]{4,3,2,1,0:T(8,128)(2,1)} %param.4) | copy-start | bytes 3342340
  42.0 4.4 %copy-start.4 = (bf16[2176,256]{1,0:T(8,128)(2,1)}, bf16[2176,256]{1,0:T(8,128)(2,1)S(1)}, u32[]{:S(2)}) copy-start(bf16[2176,256]{1,0:T(8,128)(2,1)S(1)} %fusion.9) | copy-start | bytes 3342340
  47.6 13.7 %collective-permute-start.2 = (bf16[1,17,1,64,256]{4,3,2,1,0:T(8,128)(2,1)}, bf16[1,17,1,64,256]{4,3,2,1,0:T(8,128)(2,1)}, u32[]{:S(2)}, u32[]{:S(2)}) collective-permute-start(bf16[1,17,1,64,256]{4,3,2,1,0:T(8,128)(2,1)} %get-tuple-element.6), channel_id=1, source_target_pairs={{0,1},{1,2},{2,3},{3,4},{4,5},{5,6},{6,7},{7,8},{8,9},{9,10},{10,1... | collective-permute-start | bytes 1671176 | tf_op jit(solution)/shard_map/ppermute | solution.py:15
  51.2 15.1 %collective-permute-start.3 = (bf16[1,17,1,64,256]{4,3,2,1,0:T(8,128)(2,1)}, bf16[1,17,1,64,256]{4,3,2,1,0:T(8,128)(2,1)}, u32[]{:S(2)}, u32[]{:S(2)}) collective-permute-start(bf16[1,17,1,64,256]{4,3,2,1,0:T(8,128)(2,1)} %get-tuple-element.7), channel_id=1, source_target_pairs={{1,0},{2,1},{3,2},{4,3},{5,4},{6,5},{7,6},{8,7},{9,8},{10,9},{11,1... | collective-permute-start | bytes 1671176 | tf_op jit(solution)/shard_map/ppermute | solution.py:17
  52.6 1.0 copy-start.2
  57.1 9.2 %copy-start.5 = (bf16[2176,256]{1,0:T(8,128)(2,1)S(1)}, bf16[2176,256]{1,0:T(8,128)(2,1)}, u32[]{:S(2)}) copy-start(bf16[2176,256]{1,0:T(8,128)(2,1)} %copy-done.4) | copy-start | bytes 3342340
  71.0 1.3 copy-start.7
  326.8 3.4 copy-start.9
Sparse Core Ops, SparseCore 0:
  54.7 272.0 all-reduce.6
where the time goes:
time: 338 us
  waiting for transfers between devices  266 us (79%)
  matrix products  23.6 us (7%)
  local copies, waits for them, and re-layouts  15.4 us (5%)
  between operations  14.3 us (4%)
  starting transfers between devices  10.5 us (3%)
  other arithmetic  8.16 us (2%)
    psum x1, waiting for transfers between devices, body(): lax.psum((spatial_local, temporal_local), ('dp', 'tm'))  251 us
    unnamed x37, local copies, waits for them, and re-layouts  10.1 us
    ppermute x2, waiting for transfers between devices, with_halo(): lax.ppermute(head, axis, [((i + 1) % count, i) for i in range(ends)])  9.86 us
    ppermute x2, starting transfers between devices, with_halo(): lax.ppermute(tail, axis, [(i, (i + 1) % count) for i in range(ends)])  7.93 us
    dot_general x3, matrix products, causal_mix(): jnp.dot(earlier, weight[tap], preferred_element_type=jnp.float32)  6.79 us
  transfers between devices with their start and end apart: 5, of which 5 were waited for; matrix products, arithmetic and copies ran while one was open for 6% of the time, Pallas kernels for 0%

commit v1 on v0

--- a/solution.py
+++ b/solution.py
@@ -2,6 +2,11 @@
 import jax.numpy as jnp
 from jax import lax
 from jax.sharding import PartitionSpec as P
+
+
+def side_obtain(xin):
+    local_next = lax.psum(xin, axis_name="tm")
+    return lax.psum(local_next, axis_name="dp")
 
 
 def with_halo(cells, sides, width):
@@ -101,7 +106,7 @@
     spatial_local = lax.dot_general(
         patches, pre_grad, (((0,), (0,)), ((), ())), preferred_element_type=jnp.float32
     )
-    spatial_sum, temporal_sum = lax.psum((spatial_local, temporal_local), ("dp", "tm"))
+    spatial_sum, temporal_sum = side_obtain((spatial_local, temporal_local))
     scale = (clips * lax.axis_size("dp") * frames * rows * lax.axis_size("tm") * cols) ** (-0.5)
     return (
         block_out.reshape(latents.shape),

time: 338 us -> 299 us (0.88)
  waiting for transfers between devices: 266 us -> 218 us
  local copies, waits for them, and re-layouts: 15.4 us -> 25.9 us
    psum x1 -> x2, waiting for transfers between devices: 251 us -> 190 us  [the longest x1 133 us: side_obtain(): local_next = lax.psum(xin, axis_name='tm')]
    ppermute x2, waiting for transfers between devices: 5.39 us -> 17.2 us  [with_halo(): lax.ppermute(tail, axis, [(i, (i + 1) % count) for i in range(ends)])]
    unnamed x37 -> x43, local copies, waits for them, and re-layouts: 10.1 us -> 20.1 us
    dot_general x3, matrix products: 6.79 us -> 2.38 us  [causal_mix(): jnp.dot(earlier, weight[tap], preferred_element_type=jnp.float32)]
    dot_general x1, matrix products: 3.77 us -> 7.62 us  [body(): jnp.dot(band_patches(grad_ext.reshape(clips * frames, rows + 2, cols, cha...]
  transfers between devices with their start and end apart: 5 -> 6, of which waited for: 5 -> 6; matrix products, arithmetic and copies ran while one was open for 6% -> 10% of each run, Pallas kernels for 0% -> 0%
where the time goes in v1:
time: 299 us; the launch traced here: 296 us
  waiting for transfers between devices  218 us (73%)
  local copies, waits for them, and re-layouts  25.9 us (9%)
  matrix products  21.7 us (7%)
  between operations  14.3 us (5%)
  starting transfers between devices  9.79 us (3%)
  other arithmetic  5.72 us (2%)
    psum x1, waiting for transfers between devices, side_obtain(): local_next = lax.psum(xin, axis_name='tm')  133 us
    psum x1, waiting for transfers between devices, side_obtain(): return lax.psum(local_next, axis_name='dp')  57.3 us
    unnamed x43, local copies, waits for them, and re-layouts  20.1 us
    ppermute x2, waiting for transfers between devices, with_halo(): lax.ppermute(tail, axis, [(i, (i + 1) % count) for i in range(ends)])  17.2 us
    ppermute x2, waiting for transfers between devices, with_halo(): lax.ppermute(head, axis, [((i + 1) % count, i) for i in range(ends)])  10.6 us
    dot_general x1, matrix products, body(): jnp.dot(band_patches(grad_ext.reshape(clips * frames, rows + 2, cols, cha...  7.62 us
    ppermute x2, starting transfers between devices, with_halo(): lax.ppermute(tail, axis, [(i, (i + 1) % count) for i in range(ends)])  7.13 us
  transfers between devices with their start and end apart: 6, of which 6 were waited for; matrix products, arithmetic and copies ran while one was open for 10% of the time, Pallas kernels for 0%

profile of v1, /device:TPU:2, one launch (start us, length us, event | category | flops | bytes accessed | tf_op | source)
XLA Modules:
  0.0 295.7 jit_solution(15650048487257457708)
XLA Ops:
  7.2 0.0 all-reduce.9.cloned.1.call-start
  7.2 1.4 fusion.37
  8.6 3.5 %collective-permute-start = (bf16[1,17,1,64,256]{4,3,2,1,0:T(8,128)(2,1)S(1)}, bf16[1,17,1,64,256]{4,3,2,1,0:T(8,128)(2,1)S(1)}, u32[]{:S(2)}, u32[]{:S(2)}) collective-permute-start(bf16[1,17,1,64,256]{4,3,2,1,0:T(8,128)(2,1)S(1)} %get-tuple-element.14), channel_id=1, source_target_pairs={{0,1},{1,2},{2,3},{3,4},{4,5},{5,6},{6,7},{7,8},{8,9},{9,10},{10,1... | collective-permute-start | bytes 1671176 | tf_op jit(solution)/shard_map/ppermute | solution.py:20
  12.1 1.3 collective-permute-start.1
  13.4 1.4 fusion.26
  14.8 0.0 copy-start.10
  14.8 0.2 pad_slice_fusion.12
  15.1 0.7 copy-done.10
  15.8 0.5 convolution_add_fusion.1
  16.4 7.6 %collective-permute-done = bf16[1,17,1,64,256]{4,3,2,1,0:T(8,128)(2,1)S(1)} collective-permute-done((bf16[1,17,1,64,256]{4,3,2,1,0:T(8,128)(2,1)S(1)}, bf16[1,17,1,64,256]{4,3,2,1,0:T(8,128)(2,1)S(1)}, u32[]{:S(2)}, u32[]{:S(2)}) %collective-permute-start) | collective-permute-done | bytes 557088 | tf_op jit(solution)/shard_map/ppermute | solution.py:20
  24.0 4.1 %collective-permute-done.1 = bf16[1,17,1,64,256]{4,3,2,1,0:T(8,128)(2,1)S(1)} collective-permute-done((bf16[1,17,1,64,256]{4,3,2,1,0:T(8,128)(2,1)S(1)}, bf16[1,17,1,64,256]{4,3,2,1,0:T(8,128)(2,1)S(1)}, u32[]{:S(2)}, u32[]{:S(2)}) %collective-permute-start.1) | collective-permute-done | bytes 557088 | tf_op jit(solution)/shard_map/ppermute | solution.py:22
  28.1 0.2 maximum_bitcast_fusion
  28.4 0.4 fusion.10
  28.7 0.1 slice_dynamic-update-slice_fusion.5
  28.8 0.6 fusion.11
  29.4 0.7 fusion.12
  30.1 0.1 slice_dynamic-update-slice_fusion.4
  30.2 0.6 fusion.13
  30.8 0.7 fusion.14
  31.5 0.1 slice_dynamic-update-slice_fusion.3
  31.6 0.0 copy-start.8
  31.6 0.6 fusion.15
  32.2 0.7 copy-done.8
  32.9 2.9 multiply_convert_fusion
  35.8 1.0 fusion.9
  36.9 4.4 %fusion.38 = f32[2304,256]{1,0:T(8,128)} fusion(bf16[2176,2304]{1,0:T(8,128)(2,1)S(1)} %bitcast.83, bf16[2176,256]{1,0:T(8,128)(2,1)S(1)} %fusion.9), kind=kOutput, calls=%fused_computation.75 | convolution fusion | flops 2566914048 | bytes 13500416 | tf_op jit(solution)/shard_map/dot_general | solution.py:106
  41.2 0.5 convolution_bitcast_fusion.2
  41.8 0.4 pad_slice_fusion.14
  42.2 0.0 copy-start.2
  42.2 0.0 copy-start.4
  42.2 0.5 convolution_bitcast_fusion
  42.7 0.5 convolution_bitcast_fusion.1
  43.2 0.3 copy-done.4
  43.5 0.9 pad_maximum_fusion
  44.5 0.0 all-reduce.9.cloned.1.call-update
  44.5 0.0 all-reduce.11.cloned.1.call-start
  44.5 2.4 copy.8
  47.0 1.3 fusion.36
  48.3 0.0 copy-start.5
  48.3 3.6 %collective-permute-start.2 = (bf16[1,17,1,64,256]{4,3,2,1,0:T(8,128)(2,1)S(1)}, bf16[1,17,1,64,256]{4,3,2,1,0:T(8,128)(2,1)S(1)}, u32[]{:S(2)}, u32[]{:S(2)}) collective-permute-start(bf16[1,17,1,64,256]{4,3,2,1,0:T(8,128)(2,1)S(1)} %get-tuple-element.8), channel_id=1, source_target_pairs={{0,1},{1,2},{2,3},{3,4},{4,5},{5,6},{6,7},{7,8},{8,9},{9,10},{10,1... | collective-permute-start | bytes 1671176 | tf_op jit(solution)/shard_map/ppermute | solution.py:20
  51.9 1.3 collective-permute-start.3
  53.3 0.5 fusion.28
  53.7 0.0 copy-start.3
  53.7 0.5 convolution_add_fusion.3
  54.2 0.8 copy-done.3
  55.0 1.5 fusion.4
  56.4 9.6 %collective-permute-done.2 = bf16[1,17,1,64,256]{4,3,2,1,0:T(8,128)(2,1)S(1)} collective-permute-done((bf16[1,17,1,64,256]{4,3,2,1,0:T(8,128)(2,1)S(1)}, bf16[1,17,1,64,256]{4,3,2,1,0:T(8,128)(2,1)S(1)}, u32[]{:S(2)}, u32[]{:S(2)}) %collective-permute-start.2) | collective-permute-done | bytes 557088 | tf_op jit(solution)/shard_map/ppermute | solution.py:20
  66.0 6.4 %collective-permute-done.3 = bf16[1,17,1,64,256]{4,3,2,1,0:T(8,128)(2,1)S(1)} collective-permute-done((bf16[1,17,1,64,256]{4,3,2,1,0:T(8,128)(2,1)S(1)}, bf16[1,17,1,64,256]{4,3,2,1,0:T(8,128)(2,1)S(1)}, u32[]{:S(2)}, u32[]{:S(2)}) %collective-permute-start.3) | collective-permute-done | bytes 557088 | tf_op jit(solution)/shard_map/ppermute | solution.py:22
  72.4 0.2 maximum_bitcast_fusion.1
  72.7 1.5 fusion.16
  74.1 1.2 slice_dynamic-update-slice_fusion.2
  75.3 1.8 fusion.17
  77.1 1.7 fusion.18
  78.7 1.2 slice_dynamic-update-slice_fusion.1
  79.9 133.1 %all-reduce.9.cloned.1.call-done = (f32[2304,256]{1,0:T(8,128)}, f32[3,256,256]{2,1,0:T(8,128)}) async-done(((f32[2304,256]{1,0:T(8,128)}, f32[3,256,256]{2,1,0:T(8,128)}), (f32[2304,256]{1,0:T(8,128)}, f32[3,256,256]{2,1,0:T(8,128)})) %all-reduce.9.cloned.1.call-update) | async-done | bytes 3145744 | tf_op jit(solution)/shard_map/psum | solution.py:8
  213.0 0.0 all-reduce.11.cloned.1.call-update
  213.0 1.8 fusion.19
  214.8 1.8 fusion.20
  216.6 1.2 slice_dynamic-update-slice_fusion
  217.7 1.8 fusion.21
  219.6 7.6 %fusion = bf16[2176,256]{1,0:T(8,128)(2,1)} fusion(bf16[2176,2304]{1,0:T(8,128)(2,1)} %bitcast.17, bf16[2304,256]{1,0:T(8,128)(2,1)S(1)} %bitcast.79, bf16[2176,256]{1,0:T(8,128)(2,1)S(1)} %bitcast.67), kind=kOutput, calls=%fused_computation.5 | convolution fusion | flops 2568585216 | bytes 13434880 | tf_op jit(solution)/shard_map/dot_general | solution.py:96
  227.2 57.3 %all-reduce.11.cloned.1.call-done = (f32[2304,256]{1,0:T(8,128)}, f32[3,256,256]{2,1,0:T(8,128)}) async-done(((f32[2304,256]{1,0:T(8,128)}, f32[3,256,256]{2,1,0:T(8,128)}), (f32[2304,256]{1,0:T(8,128)}, f32[3,256,256]{2,1,0:T(8,128)})) %all-reduce.11.cloned.1.call-update) | async-done | bytes 3145744 | tf_op jit(solution)/shard_map/psum | solution.py:9
  284.5 3.3 %broadcast_multiply_fusion = f32[2304,256]{1,0:T(8,128)} fusion(f32[2304,256]{1,0:T(8,128)} %get-tuple-element.6), kind=kLoop, calls=%fused_computation.31 | loop fusion | flops 589824 | bytes 4718592 | tf_op jit(solution)/shard_map/mul | solution.py:114
  287.9 0.9 broadcast_multiply_fusion.1
  (16 shorter events, 0.0 us)
Async XLA Ops:
  7.2 6.3 %copy-start = (bf16[1,17,2,64,256]{4,3,2,1,0:T(8,128)(2,1)S(1)}, bf16[1,17,2,64,256]{4,3,2,1,0:T(8,128)(2,1)}, u32[]{:S(2)}) copy-start(bf16[1,17,2,64,256]{4,3,2,1,0:T(8,128)(2,1)} %param.5) | copy-start | bytes 3342340
  7.2 205.8 %all-reduce.9.cloned.1.call-start = ((), (), s32[]{:S(2)}) async-start(), calls=%async_computation | async-start | bytes 6291456 | tf_op jit(solution)/shard_map/psum | solution.py:8
  8.6 15.4 %collective-permute-start = (bf16[1,17,1,64,256]{4,3,2,1,0:T(8,128)(2,1)S(1)}, bf16[1,17,1,64,256]{4,3,2,1,0:T(8,128)(2,1)S(1)}, u32[]{:S(2)}, u32[]{:S(2)}) collective-permute-start(bf16[1,17,1,64,256]{4,3,2,1,0:T(8,128)(2,1)S(1)} %get-tuple-element.14), channel_id=1, source_target_pairs={{0,1},{1,2},{2,3},{3,4},{4,5},{5,6},{6,7},{7,8},{8,9},{9,10},{10,1... | collective-permute-start | bytes 1671176 | tf_op jit(solution)/shard_map/ppermute | solution.py:20
  12.1 16.0 %collective-permute-start.1 = (bf16[1,17,1,64,256]{4,3,2,1,0:T(8,128)(2,1)S(1)}, bf16[1,17,1,64,256]{4,3,2,1,0:T(8,128)(2,1)S(1)}, u32[]{:S(2)}, u32[]{:S(2)}) collective-permute-start(bf16[1,17,1,64,256]{4,3,2,1,0:T(8,128)(2,1)S(1)} %get-tuple-element.15), channel_id=1, source_target_pairs={{1,0},{2,1},{3,2},{4,3},{5,4},{6,5},{7,6},{8,7},{9,8},{10,9},{11,1... | collective-permute-start | bytes 1671176 | tf_op jit(solution)/shard_map/ppermute | solution.py:22
  14.8 1.0 copy-start.10
  15.8 12.3 %copy-start.1 = (bf16[1,17,2,64,256]{4,3,2,1,0:T(8,128)(2,1)S(1)}, bf16[1,17,2,64,256]{4,3,2,1,0:T(8,128)(2,1)}, u32[]{:S(2)}) copy-start(bf16[1,17,2,64,256]{4,3,2,1,0:T(8,128)(2,1)} %param.4) | copy-start | bytes 3342340
  31.6 1.3 copy-start.8
  36.8 4.4 %copy-start.6 = (bf16[2176,256]{1,0:T(8,128)(2,1)}, bf16[2176,256]{1,0:T(8,128)(2,1)S(1)}, u32[]{:S(2)}) copy-start(bf16[2176,256]{1,0:T(8,128)(2,1)S(1)} %fusion.9) | copy-start | bytes 3342340
  42.2 1.1 copy-start.2
  42.2 1.4 copy-start.4
  44.5 240.1 %all-reduce.11.cloned.1.call-start = ((), (), s32[]{:S(2)}) async-start(), calls=%async_computation.1 | async-start | bytes 6291456 | tf_op jit(solution)/shard_map/psum | solution.py:9
  47.0 6.3 %copy-start.11 = (bf16[3,256,256]{2,1,0:T(8,128)(2,1)S(1)}, bf16[3,256,256]{2,1,0:T(8,128)(2,1)}, u32[]{:S(2)}) copy-start(bf16[3,256,256]{2,1,0:T(8,128)(2,1)} %param.7) | copy-start | bytes 1179652
  48.3 5.4 %copy-start.5 = (bf16[1,17,128,256]{3,2,1,0:T(8,128)(2,1)S(1)}, bf16[1,17,128,256]{3,2,1,0:T(8,128)(2,1)}, u32[]{:S(2)}) copy-start(bf16[1,17,128,256]{3,2,1,0:T(8,128)(2,1)} %copy-done.4) | copy-start | bytes 3342340
  48.3 17.7 %collective-permute-start.2 = (bf16[1,17,1,64,256]{4,3,2,1,0:T(8,128)(2,1)S(1)}, bf16[1,17,1,64,256]{4,3,2,1,0:T(8,128)(2,1)S(1)}, u32[]{:S(2)}, u32[]{:S(2)}) collective-permute-start(bf16[1,17,1,64,256]{4,3,2,1,0:T(8,128)(2,1)S(1)} %get-tuple-element.8), channel_id=1, source_target_pairs={{0,1},{1,2},{2,3},{3,4},{4,5},{5,6},{6,7},{7,8},{8,9},{9,10},{10,1... | collective-permute-start | bytes 1671176 | tf_op jit(solution)/shard_map/ppermute | solution.py:20
  51.9 20.5 %collective-permute-start.3 = (bf16[1,17,1,64,256]{4,3,2,1,0:T(8,128)(2,1)S(1)}, bf16[1,17,1,64,256]{4,3,2,1,0:T(8,128)(2,1)S(1)}, u32[]{:S(2)}, u32[]{:S(2)}) collective-permute-start(bf16[1,17,1,64,256]{4,3,2,1,0:T(8,128)(2,1)S(1)} %get-tuple-element.9), channel_id=1, source_target_pairs={{1,0},{2,1},{3,2},{4,3},{5,4},{6,5},{7,6},{8,7},{9,8},{10,9},{11,1... | collective-permute-start | bytes 1671176 | tf_op jit(solution)/shard_map/ppermute | solution.py:22
  53.7 1.3 copy-start.3
  55.0 17.4 %copy-start.7 = (bf16[2176,256]{1,0:T(8,128)(2,1)S(1)}, bf16[2176,256]{1,0:T(8,128)(2,1)}, u32[]{:S(2)}) copy-start(bf16[2176,256]{1,0:T(8,128)(2,1)} %copy-done.6) | copy-start | bytes 3342340
  217.7 1.8 copy-start.9
  284.5 3.4 %copy-start.12 = (f32[3,256,256]{2,1,0:T(8,128)S(1)}, f32[3,256,256]{2,1,0:T(8,128)}, u32[]{:S(2)}) copy-start(f32[3,256,256]{2,1,0:T(8,128)} %get-tuple-element.7) | copy-start | bytes 2359300
Sparse Core Ops, SparseCore 0:
  44.6 168.3 all-reduce.8
  215.5 68.9 all-reduce.10
